TPU v7x, 32 devices: a whole 2x2x4 slice. The times are simulated.
32 devices in a mesh: groups: 2 (over x), blocks: 16 (over z, y, core).
Axes of the slice: x: 2, y: 2, z: 4, core: 2. Of those that a mesh axis runs over, the one named last changes fastest.
Arguments:
- activations: float32 [2048, 2048], P('blocks', 'groups'), parts along dimension 1, may hold values from -180 to 180
- cotangent: float32 [2048, 2048], P('blocks', 'groups'), parts along dimension 1, may hold values from -6 to 6
- gain: float32 [2048], P('blocks'), may hold values from 0.5 to 1.5
- left_one: float32 [16, 128, 128], P('blocks'), may hold values from -0.5 to 0.5
- right_one: float32 [128, 16, 16], P('blocks'), may hold values from -1.5 to 1.5
- left_two: float32 [16, 128, 128], P('blocks'), may hold values from -0.5 to 0.5
- right_two: float32 [128, 16, 16], P('blocks'), may hold values from -1.5 to 1.5
Outputs:
- output: float32 [2048, 2048], P('blocks', 'groups'), parts along dimension 1
- input_gradient: float32 [2048, 2048], P('blocks', 'groups'), parts along dimension 1
- gain_gradient: float32 [4096], P(('groups', 'blocks')), parts along dimension 0
- grad_left_one: float32 [32, 128, 128], P(('groups', 'blocks')), parts along dimension 0
- grad_right_one: float32 [256, 16, 16], P(('groups', 'blocks')), parts along dimension 0
- grad_left_two: float32 [32, 128, 128], P(('groups', 'blocks')), parts along dimension 0
- grad_right_two: float32 [256, 16, 16], P(('groups', 'blocks')), parts along dimension 0
There are 2 independent parts, one for each index of `groups`. A program takes and returns all parts, laid end to end along the dimension named above; an argument that names none is the same for every part. Nothing has to cross between parts.
All inputs are finite; a program needn't handle non-finite values.
Results may differ from a plain program's by a relative error of at most 0.0001.
Values sent between devices are 32-bit elements; how exact they have to be, the bound alone decides.
No kernel may reach another device: no remote copies, remote signals or barrier semaphores. Data moves between devices by JAX's collectives and lax.ppermute only.
A program may use at most 64 MiB of HBM per device.

v0:
```python
import math
import jax
import jax.numpy as jnp
from jax import lax
from jax.sharding import PartitionSpec as P

COEFF = math.sqrt(2.0 / math.pi)
EPSILON = 1e-05
HIGH = lax.Precision.HIGHEST


def gelu_value(values):
    return 0.5 * values * (1.0 + jnp.tanh(COEFF * (values + 0.044715 * values * values * values)))


def gelu_slope(values):
    tangent = jnp.tanh(COEFF * (values + 0.044715 * values * values * values))
    return 0.5 * (1.0 + tangent) + 0.5 * values * (1.0 - tangent * tangent) * COEFF * (
        1.0 + 3.0 * 0.044715 * values * values
    )


def first_factor(stacked, left):
    return jnp.einsum("bij,bit->bjt", left, stacked, precision=HIGH)


def monarch_forward(stacked, left, right):
    first = first_factor(stacked, left)
    regrouped = lax.all_to_all(first, "blocks", split_axis=1, concat_axis=0, tiled=True)
    second = jnp.einsum("jbk,bjt->jkt", right, regrouped, precision=HIGH)
    return (second, regrouped)


def monarch_backward(grad_out, stacked, left, right, regrouped, factor_matrix):
    grad_right = jnp.einsum("bjt,jkt->jbk", regrouped, grad_out, precision=HIGH) * factor_matrix
    grad_mid = jnp.einsum("jbk,jkt->bjt", right, grad_out, precision=HIGH)
    piece = lax.all_to_all(grad_mid, "blocks", split_axis=0, concat_axis=1, tiled=True)
    grad_stacked = jnp.einsum("bij,bjt->bit", left, piece, precision=HIGH)
    grad_left = jnp.einsum("bit,bjt->bij", stacked, piece, precision=HIGH) * factor_matrix
    return (grad_stacked, grad_left, grad_right)


def local(activations, cotangent, gain, left_one, right_one, left_two, right_two):
    features, tokens = activations.shape
    blocks_here = left_one.shape[0]
    block_order = left_one.shape[1]
    outer_here = right_one.shape[0]
    block_count = right_one.shape[1]
    feature_width = features * lax.axis_size("blocks")
    factor_matrix = tokens ** (-0.5)
    squares = lax.psum(jnp.sum(activations * activations, axis=0), "blocks")
    inverse_root = lax.rsqrt(squares / feature_width + EPSILON)[None, :]
    centered_input = activations * inverse_root
    normed_rows = centered_input * gain[:, None]
    normed_stacked = normed_rows.reshape(blocks_here, block_order, tokens)
    second_one, regrouped_one = monarch_forward(normed_stacked, left_one, right_one)
    pre = second_one.reshape(features, tokens)
    acted = gelu_value(pre)
    acted_stacked = acted.reshape(blocks_here, block_order, tokens)
    second_two, regrouped_two = monarch_forward(acted_stacked, left_two, right_two)
    output = activations + second_two.reshape(features, tokens)
    grad_acted, grad_left_two, grad_right_two = monarch_backward(
        cotangent.reshape(outer_here, block_count, tokens),
        acted_stacked,
        left_two,
        right_two,
        regrouped_two,
        factor_matrix,
    )
    grad_pre = grad_acted.reshape(features, tokens) * gelu_slope(pre)
    normalized_gradient, grad_left_one, grad_right_one = monarch_backward(
        grad_pre.reshape(outer_here, block_count, tokens),
        normed_stacked,
        left_one,
        right_one,
        regrouped_one,
        factor_matrix,
    )
    normalized_gradient = normalized_gradient.reshape(features, tokens)
    gradient_scaled = gain[:, None] * normalized_gradient
    inner_width = lax.psum(jnp.sum(gradient_scaled * centered_input, axis=0), "blocks")
    input_gradient = cotangent + inverse_root * (
        gradient_scaled - centered_input * (inner_width / feature_width)[None, :]
    )
    gain_gradient = jnp.sum(normalized_gradient * centered_input, axis=1) * factor_matrix
    return (
        output,
        input_gradient,
        gain_gradient,
        grad_left_one,
        grad_right_one,
        grad_left_two,
        grad_right_two,
    )


def solution(mesh):
    return jax.shard_map(
        local,
        mesh=mesh,
        in_specs=(
            P("blocks", "groups"),
            P("blocks", "groups"),
            P("blocks"),
            P("blocks", None, None),
            P("blocks", None, None),
            P("blocks", None, None),
            P("blocks", None, None),
        ),
        out_specs=(
            P("blocks", "groups"),
            P("blocks", "groups"),
            P(("groups", "blocks")),
            P(("groups", "blocks"), None, None),
            P(("groups", "blocks"), None, None),
            P(("groups", "blocks"), None, None),
            P(("groups", "blocks"), None, None),
        ),
        check_vma=False,
    )
```

profile of v0, /device:TPU:0, one launch (start us, length us, event | category | flops | bytes accessed | tf_op | source)
XLA Modules:
  0.0 149.8 jit_solution(11019445430799419862)
XLA Ops:
  0.7 1.2 multiply_reduce_fusion.2
  2.1 35.0 %psum.14 = f32[1024]{0:T(1024)S(1)} all-reduce(f32[1024]{0:T(1024)S(1)} %multiply_reduce_fusion.2), channel_id=1, replica_groups=mesh['groups'=2,'blocks'=16] {'blocks'}, use_global_device_ids=true, to_apply=%region_1.0 | all-reduce | flops 1024 | bytes 8192 | tf_op jit(solution)/shard_map/psum | solution.py:51
  38.3 1.0 copy.37
  39.4 3.7 %all-to-all-start = ((f32[1,128,1024]{2,0,1:T(1,128)}), f32[1,128,1024]{2,0,1:T(1,128)S(1)}, u32[]{:S(2)}, u32[]{:S(2)}) async-start(f32[1,128,1024]{2,0,1:T(1,128)} %copy.37), calls=%async_computation | async-start | bytes 1048576 | tf_op jit(solution)/shard_map/all_to_all | solution.py:29
  43.7 1.1 copy.43
  44.8 12.5 %all-to-all-done = f32[1,128,1024]{2,0,1:T(1,128)S(1)} async-done(((f32[1,128,1024]{2,0,1:T(1,128)}), f32[1,128,1024]{2,0,1:T(1,128)S(1)}, u32[]{:S(2)}, u32[]{:S(2)}) %all-to-all-start) | async-done | bytes 524320 | tf_op jit(solution)/shard_map/all_to_all | solution.py:29
  57.3 4.1 %all-to-all-start.2 = ((f32[16,8,1024]{2,1,0:T(8,128)}), f32[16,8,1024]{2,1,0:T(8,128)S(1)}, u32[]{:S(2)}, u32[]{:S(2)}) async-start(f32[16,8,1024]{2,1,0:T(8,128)} %copy.43), calls=%async_computation.2 | async-start | bytes 1048576 | tf_op jit(solution)/shard_map/all_to_all | solution.py:37
  61.6 1.8 %add_multiply_fusion = (f32[8,16,1024]{2,1,0:T(8,128)S(1)}, f32[8,16,1024]{2,1,0:T(8,128)}) fusion(f32[8,16,16]{2,1,0:T(8,128)S(1)} %copy-done, f32[16,8,1024]{2,1,0:T(8,128)S(1)} %bitcast.73), kind=kOutput, calls=%fused_computation.37 | convolution fusion | flops 26214400 | bytes 1581056 | tf_op jit(solution)/shard_map/jbk,bjt->jkt/dot_general | solution.py:30
  63.4 1.0 convolution_bitcast_fusion.3
  64.4 1.0 copy.40
  65.4 10.3 %all-to-all-done.2 = f32[16,8,1024]{2,1,0:T(8,128)S(1)} async-done(((f32[16,8,1024]{2,1,0:T(8,128)}), f32[16,8,1024]{2,1,0:T(8,128)S(1)}, u32[]{:S(2)}, u32[]{:S(2)}) %all-to-all-start.2) | async-done | bytes 524320 | tf_op jit(solution)/shard_map/all_to_all | solution.py:37
  75.7 4.2 %all-to-all-start.1 = ((f32[1,128,1024]{2,0,1:T(1,128)}), f32[1,128,1024]{2,0,1:T(1,128)}, u32[]{:S(2)}, u32[]{:S(2)}) async-start(f32[1,128,1024]{2,0,1:T(1,128)} %copy.40), calls=%async_computation.1 | async-start | bytes 1048576 | tf_op jit(solution)/shard_map/all_to_all | solution.py:29
  82.1 1.1 copy.44
  83.2 1.2 fusion
  84.4 9.8 %all-to-all-done.1 = f32[1,128,1024]{2,0,1:T(1,128)} async-done(((f32[1,128,1024]{2,0,1:T(1,128)}), f32[1,128,1024]{2,0,1:T(1,128)}, u32[]{:S(2)}, u32[]{:S(2)}) %all-to-all-start.1) | async-done | bytes 524320 | tf_op jit(solution)/shard_map/all_to_all | solution.py:29
  94.2 4.2 %all-to-all-start.3 = ((f32[16,8,1024]{2,1,0:T(8,128)}), f32[16,8,1024]{2,1,0:T(8,128)S(1)}, u32[]{:S(2)}, u32[]{:S(2)}) async-start(f32[16,8,1024]{2,1,0:T(8,128)} %copy.44), calls=%async_computation.3 | async-start | bytes 1048576 | tf_op jit(solution)/shard_map/all_to_all | solution.py:37
  98.4 3.1 %convolution_multiply_fusion.2 = f32[8,16,16]{2,1,0:T(8,128)} fusion(f32[16,8,1024]{2,1,0:T(8,128)S(1)} %bitcast.74, f32[8,16,1024]{2,1,0:T(8,128)} %bitcast.76, f32[8,16,1024]{2,1,0:T(8,128)} %get-tuple-element.31), kind=kOutput, calls=%fused_computation.9 | convolution fusion | flops 27527168 | bytes 1581056 | tf_op jit(solution)/shard_map/bjt,jkt->jbk/dot_general | solution.py:35
  101.6 1.1 copy.65
  102.7 1.8 %convolution_multiply_fusion = f32[8,16,16]{2,1,0:T(8,128)} fusion(f32[8,16,1024]{2,1,0:T(8,128)S(1)} %bitcast.70, f32[16,8,1024]{2,1,0:T(8,128)S(1)} %bitcast.71), kind=kOutput, calls=%fused_computation.6 | convolution fusion | flops 25167872 | bytes 1056768 | tf_op jit(solution)/shard_map/bjt,jkt->jbk/dot_general | solution.py:35
  106.2 6.4 %all-to-all-done.3 = f32[16,8,1024]{2,1,0:T(8,128)S(1)} async-done(((f32[16,8,1024]{2,1,0:T(8,128)}), f32[16,8,1024]{2,1,0:T(8,128)S(1)}, u32[]{:S(2)}, u32[]{:S(2)}) %all-to-all-start.3) | async-done | bytes 524320 | tf_op jit(solution)/shard_map/all_to_all | solution.py:37
  112.7 1.2 multiply_reduce_fusion
  114.4 32.2 %psum.15 = f32[1024]{0:T(1024)S(1)} all-reduce(f32[1024]{0:T(1024)S(1)} %get-tuple-element.29), channel_id=1, replica_groups=mesh['groups'=2,'blocks'=16] {'blocks'}, use_global_device_ids=true, to_apply=%region_3.0 | all-reduce | flops 1024 | bytes 8192 | tf_op jit(solution)/shard_map/psum | solution.py:81
  147.0 1.0 copy.48
  148.0 1.8 %fusion.1 = f32[1,128,128]{2,1,0:T(8,128)} fusion(f32[16,8,1024]{2,1,0:T(8,128)S(1)} %all-to-all-done.3, f32[128,1024]{0,1:T(8,128)S(1)} %copy.36, f32[128]{0:T(128)S(1)} %copy-done.10, f32[1024]{0:T(1024)S(1)} %add_rsqrt_fusion), kind=kOutput, calls=%fused_computation.11 | convolution fusion | flops 201605120 | bytes 1118720 | tf_op jit(solution)/shard_map/bit,bjt->bij/dot_general | solution.py:39
  (35 shorter events, 7.0 us)
Async XLA Ops:
  0.6 60.9 %copy-start = (f32[8,16,16]{2,1,0:T(8,128)S(1)}, f32[8,16,16]{2,1,0:T(8,128)}, u32[]{:S(2)}) copy-start(f32[8,16,16]{2,1,0:T(8,128)} %param.11) | copy-start | bytes 24580
  0.6 1.2 copy-start.1
  1.9 35.2 %copy-start.9 = (f32[1,128,128]{2,1,0:T(8,128)S(1)}, f32[1,128,128]{2,1,0:T(8,128)}, u32[]{:S(2)}) copy-start(f32[1,128,128]{2,1,0:T(8,128)} %param.10) | copy-start | bytes 196612
  37.0 0.7 copy-start.10
  39.4 3.7 %copy-start.2 = (f32[128,1024]{1,0:T(8,128)S(1)}, f32[128,1024]{1,0:T(8,128)}, u32[]{:S(2)}) copy-start(f32[128,1024]{1,0:T(8,128)} %param.8) | copy-start | bytes 1572868
  39.4 3.7 %copy-start.8 = (f32[8,16,16]{2,1,0:T(8,128)S(1)}, f32[8,16,16]{2,1,0:T(8,128)}, u32[]{:S(2)}) copy-start(f32[8,16,16]{2,1,0:T(8,128)} %param.13) | copy-start | bytes 24580
  39.4 17.9 %all-to-all-start = ((f32[1,128,1024]{2,0,1:T(1,128)}), f32[1,128,1024]{2,0,1:T(1,128)S(1)}, u32[]{:S(2)}, u32[]{:S(2)}) async-start(f32[1,128,1024]{2,0,1:T(1,128)} %copy.37), calls=%async_computation | async-start | bytes 1048576 | tf_op jit(solution)/shard_map/all_to_all | solution.py:29
  57.3 18.4 %all-to-all-start.2 = ((f32[16,8,1024]{2,1,0:T(8,128)}), f32[16,8,1024]{2,1,0:T(8,128)S(1)}, u32[]{:S(2)}, u32[]{:S(2)}) async-start(f32[16,8,1024]{2,1,0:T(8,128)} %copy.43), calls=%async_computation.2 | async-start | bytes 1048576 | tf_op jit(solution)/shard_map/all_to_all | solution.py:37
  61.5 1.8 %copy-start.3 = (f32[1,128,1024]{2,1,0:T(8,128)}, f32[1,128,1024]{2,1,0:T(8,128)S(1)}, u32[]{:S(2)}) copy-start(f32[1,128,1024]{2,1,0:T(8,128)S(1)} %copy.66) | copy-start | bytes 1572868
  61.5 1.8 %copy-start.7 = (f32[1,128,128]{2,1,0:T(8,128)S(1)}, f32[1,128,128]{2,1,0:T(8,128)}, u32[]{:S(2)}) copy-start(f32[1,128,128]{2,1,0:T(8,128)} %param.12) | copy-start | bytes 196612
  75.7 18.5 %all-to-all-start.1 = ((f32[1,128,1024]{2,0,1:T(1,128)}), f32[1,128,1024]{2,0,1:T(1,128)}, u32[]{:S(2)}, u32[]{:S(2)}) async-start(f32[1,128,1024]{2,0,1:T(1,128)} %copy.40), calls=%async_computation.1 | async-start | bytes 1048576 | tf_op jit(solution)/shard_map/all_to_all | solution.py:29
  80.1 1.0 copy-start.5
  80.8 1.3 copy-start.6
  84.4 14.0 %copy-start.4 = (f32[1,128,1024]{2,1,0:T(8,128)S(1)}, f32[1,128,1024]{2,1,0:T(8,128)}, u32[]{:S(2)}) copy-start(f32[1,128,1024]{2,1,0:T(8,128)} %copy-done.3) | copy-start | bytes 1572868
  94.2 18.4 %all-to-all-start.3 = ((f32[16,8,1024]{2,1,0:T(8,128)}), f32[16,8,1024]{2,1,0:T(8,128)S(1)}, u32[]{:S(2)}, u32[]{:S(2)}) async-start(f32[16,8,1024]{2,1,0:T(8,128)} %copy.44), calls=%async_computation.3 | async-start | bytes 1048576 | tf_op jit(solution)/shard_map/all_to_all | solution.py:37
where the time goes:
time: 151 us; the launch traced here: 150 us
  blocking collectives  67.2 us (45%)
  waiting for transfers between devices  39.1 us (26%)
  starting transfers between devices  16.2 us (11%)
  matrix products  15.5 us (10%)
  local copies, waits for them, and re-layouts  8.06 us (5%)
  other arithmetic  2.89 us (2%)
    psum x1, blocking collectives, local(): squares = lax.psum(jnp.sum(activations * activations, axis=0), 'blocks')  35 us
    psum x1, blocking collectives, local(): lax.psum(jnp.sum(gradient_scaled * centered_input, axis=0), 'blocks')  32.2 us
    all_to_all x2, waiting for transfers between devices, monarch_forward(): lax.all_to_all(first, 'blocks', split_axis=1, concat_axis=0, tiled=True)  22.3 us
    all_to_all x2, waiting for transfers between devices, monarch_backward(): lax.all_to_all(grad_mid, 'blocks', split_axis=0, concat_axis=1, tiled=True)  16.7 us
    all_to_all x2, starting transfers between devices, monarch_backward(): lax.all_to_all(grad_mid, 'blocks', split_axis=0, concat_axis=1, tiled=True)  8.26 us
    all_to_all x2, starting transfers between devices, monarch_forward(): lax.all_to_all(first, 'blocks', split_axis=1, concat_axis=0, tiled=True)  7.95 us
    dot_general x2, matrix products, monarch_backward(): jnp.einsum('bjt,jkt->jbk', regrouped, grad_out, precision=HIGH)  4.91 us
    unnamed x27, local copies, waits for them, and re-layouts  3.76 us
  transfers between devices with their start and end apart: 4, of which 4 were waited for; matrix products, arithmetic and copies ran while one was open for 12% of the time, Pallas kernels for 0%

commit v1 on v0

--- a/solution.py
+++ b/solution.py
@@ -78,7 +78,9 @@
     )
     normalized_gradient = normalized_gradient.reshape(features, tokens)
     gradient_scaled = gain[:, None] * normalized_gradient
-    inner_width = lax.psum(jnp.sum(gradient_scaled * centered_input, axis=0), "blocks")
+    inner_width = jnp.sum(
+        lax.all_gather(jnp.sum(gradient_scaled * centered_input, axis=0), "blocks"), axis=0
+    )
     input_gradient = cotangent + inverse_root * (
         gradient_scaled - centered_input * (inner_width / feature_width)[None, :]
     )

time: 151 us -> 138 us (0.914)
  blocking collectives: 67.2 us -> 55 us
    psum x1 -> x0, blocking collectives: 32.2 us -> none  [local(): lax.psum(jnp.sum(gradient_scaled * centered_input, axis=0), 'blocks')]
    all_gather x0 -> x1, blocking collectives: none -> 20 us  [local(): lax.all_gather(jnp.sum(gradient_scaled * centered_input, axis=0), 'blocks')]
  transfers between devices with their start and end apart: 4 -> 4, of which waited for: 4 -> 4; matrix products, arithmetic and copies ran while one was open for 12% -> 13% of each run, Pallas kernels for 0% -> 0%
where the time goes in v1:
time: 138 us
  blocking collectives  55 us (40%)
  waiting for transfers between devices  39.1 us (28%)
  starting transfers between devices  16.2 us (12%)
  matrix products  15.5 us (11%)
  local copies, waits for them, and re-layouts  8.07 us (6%)
  other arithmetic  2.9 us (2%)
    psum x1, blocking collectives, local(): squares = lax.psum(jnp.sum(activations * activations, axis=0), 'blocks')  35 us
    all_to_all x2, waiting for transfers between devices, monarch_forward(): lax.all_to_all(first, 'blocks', split_axis=1, concat_axis=0, tiled=True)  22.3 us
    all_gather x1, blocking collectives, local(): lax.all_gather(jnp.sum(gradient_scaled * centered_input, axis=0), 'blocks')  20 us
    all_to_all x2, waiting for transfers between devices, monarch_backward(): lax.all_to_all(grad_mid, 'blocks', split_axis=0, concat_axis=1, tiled=True)  16.7 us
    all_to_all x2, starting transfers between devices, monarch_backward(): lax.all_to_all(grad_mid, 'blocks', split_axis=0, concat_axis=1, tiled=True)  8.26 us
    all_to_all x2, starting transfers between devices, monarch_forward(): lax.all_to_all(first, 'blocks', split_axis=1, concat_axis=0, tiled=True)  7.95 us
    dot_general x2, matrix products, monarch_backward(): jnp.einsum('bjt,jkt->jbk', regrouped, grad_out, precision=HIGH)  4.91 us
    unnamed x27, local copies, waits for them, and re-layouts  3.76 us
  transfers between devices with their start and end apart: 4, of which 4 were waited for; matrix products, arithmetic and copies ran while one was open for 13% of the time, Pallas kernels for 0%

profile of v1, /device:TPU:0, one launch (start us, length us, event | category | flops | bytes accessed | tf_op | source)
XLA Modules:
  0.0 137.6 jit_solution(9901189688500936383)
XLA Ops:
  0.7 1.2 multiply_reduce_fusion.2
  2.1 35.0 %psum.7 = f32[1024]{0:T(1024)S(1)} all-reduce(f32[1024]{0:T(1024)S(1)} %multiply_reduce_fusion.2), channel_id=1, replica_groups=mesh['groups'=2,'blocks'=16] {'blocks'}, use_global_device_ids=true, to_apply=%region_1.0 | all-reduce | flops 1024 | bytes 8192 | tf_op jit(solution)/shard_map/psum | solution.py:51
  38.3 1.0 copy.50
  39.4 3.7 %all-to-all-start = ((f32[1,128,1024]{2,0,1:T(1,128)}), f32[1,128,1024]{2,0,1:T(1,128)S(1)}, u32[]{:S(2)}, u32[]{:S(2)}) async-start(f32[1,128,1024]{2,0,1:T(1,128)} %copy.50), calls=%async_computation | async-start | bytes 1048576 | tf_op jit(solution)/shard_map/all_to_all | solution.py:29
  43.7 1.1 copy.56
  44.8 12.5 %all-to-all-done = f32[1,128,1024]{2,0,1:T(1,128)S(1)} async-done(((f32[1,128,1024]{2,0,1:T(1,128)}), f32[1,128,1024]{2,0,1:T(1,128)S(1)}, u32[]{:S(2)}, u32[]{:S(2)}) %all-to-all-start) | async-done | bytes 524320 | tf_op jit(solution)/shard_map/all_to_all | solution.py:29
  57.3 4.1 %all-to-all-start.2 = ((f32[16,8,1024]{2,1,0:T(8,128)}), f32[16,8,1024]{2,1,0:T(8,128)S(1)}, u32[]{:S(2)}, u32[]{:S(2)}) async-start(f32[16,8,1024]{2,1,0:T(8,128)} %copy.56), calls=%async_computation.2 | async-start | bytes 1048576 | tf_op jit(solution)/shard_map/all_to_all | solution.py:37
  61.6 1.8 %add_multiply_fusion = (f32[8,16,1024]{2,1,0:T(8,128)S(1)}, f32[8,16,1024]{2,1,0:T(8,128)}) fusion(f32[8,16,16]{2,1,0:T(8,128)S(1)} %copy-done, f32[16,8,1024]{2,1,0:T(8,128)S(1)} %bitcast.73), kind=kOutput, calls=%fused_computation.37 | convolution fusion | flops 26214400 | bytes 1581056 | tf_op jit(solution)/shard_map/jbk,bjt->jkt/dot_general | solution.py:30
  63.4 1.0 convolution_bitcast_fusion.3
  64.4 1.0 copy.53
  65.4 10.3 %all-to-all-done.2 = f32[16,8,1024]{2,1,0:T(8,128)S(1)} async-done(((f32[16,8,1024]{2,1,0:T(8,128)}), f32[16,8,1024]{2,1,0:T(8,128)S(1)}, u32[]{:S(2)}, u32[]{:S(2)}) %all-to-all-start.2) | async-done | bytes 524320 | tf_op jit(solution)/shard_map/all_to_all | solution.py:37
  75.7 4.2 %all-to-all-start.1 = ((f32[1,128,1024]{2,0,1:T(1,128)}), f32[1,128,1024]{2,0,1:T(1,128)}, u32[]{:S(2)}, u32[]{:S(2)}) async-start(f32[1,128,1024]{2,0,1:T(1,128)} %copy.53), calls=%async_computation.1 | async-start | bytes 1048576 | tf_op jit(solution)/shard_map/all_to_all | solution.py:29
  82.1 1.1 copy.57
  83.2 1.2 fusion
  84.4 9.8 %all-to-all-done.1 = f32[1,128,1024]{2,0,1:T(1,128)} async-done(((f32[1,128,1024]{2,0,1:T(1,128)}), f32[1,128,1024]{2,0,1:T(1,128)}, u32[]{:S(2)}, u32[]{:S(2)}) %all-to-all-start.1) | async-done | bytes 524320 | tf_op jit(solution)/shard_map/all_to_all | solution.py:29
  94.2 4.2 %all-to-all-start.3 = ((f32[16,8,1024]{2,1,0:T(8,128)}), f32[16,8,1024]{2,1,0:T(8,128)S(1)}, u32[]{:S(2)}, u32[]{:S(2)}) async-start(f32[16,8,1024]{2,1,0:T(8,128)} %copy.57), calls=%async_computation.3 | async-start | bytes 1048576 | tf_op jit(solution)/shard_map/all_to_all | solution.py:37
  98.4 3.1 %convolution_multiply_fusion.2 = f32[8,16,16]{2,1,0:T(8,128)} fusion(f32[16,8,1024]{2,1,0:T(8,128)S(1)} %bitcast.74, f32[8,16,1024]{2,1,0:T(8,128)} %bitcast.76, f32[8,16,1024]{2,1,0:T(8,128)} %get-tuple-element.38), kind=kOutput, calls=%fused_computation.9 | convolution fusion | flops 27527168 | bytes 1581056 | tf_op jit(solution)/shard_map/bjt,jkt->jbk/dot_general | solution.py:35
  101.6 1.1 copy.78
  102.7 1.8 %convolution_multiply_fusion = f32[8,16,16]{2,1,0:T(8,128)} fusion(f32[8,16,1024]{2,1,0:T(8,128)S(1)} %bitcast.70, f32[16,8,1024]{2,1,0:T(8,128)S(1)} %bitcast.71), kind=kOutput, calls=%fused_computation.6 | convolution fusion | flops 25167872 | bytes 1056768 | tf_op jit(solution)/shard_map/bjt,jkt->jbk/dot_general | solution.py:35
  106.2 6.4 %all-to-all-done.3 = f32[16,8,1024]{2,1,0:T(8,128)S(1)} async-done(((f32[16,8,1024]{2,1,0:T(8,128)}), f32[16,8,1024]{2,1,0:T(8,128)S(1)}, u32[]{:S(2)}, u32[]{:S(2)}) %all-to-all-start.3) | async-done | bytes 524320 | tf_op jit(solution)/shard_map/all_to_all | solution.py:37
  112.7 1.2 multiply_reduce_fusion
  114.4 20.0 %all-gather = f32[16384]{0:T(1024)S(1)} all-gather(f32[1024]{0:T(1024)S(1)} %get-tuple-element.36), channel_id=2, replica_groups=mesh['groups'=2,'blocks'=16] {'blocks'}, dimensions={0}, use_global_device_ids=true | all-gather | bytes 69632 | tf_op jit(solution)/shard_map/all_gather | solution.py:82
  134.8 1.0 copy.61
  135.8 1.8 %fusion.1 = f32[1,128,128]{2,1,0:T(8,128)} fusion(f32[16,8,1024]{2,1,0:T(8,128)S(1)} %all-to-all-done.3, f32[128,1024]{0,1:T(8,128)S(1)} %copy.49, f32[128]{0:T(128)S(1)} %copy-done.10, f32[1024]{0:T(1024)S(1)} %add_rsqrt_fusion), kind=kOutput, calls=%fused_computation.11 | convolution fusion | flops 201605120 | bytes 1118720 | tf_op jit(solution)/shard_map/bit,bjt->bij/dot_general | solution.py:39
  (37 shorter events, 7.0 us)
Async XLA Ops:
  0.6 60.9 %copy-start = (f32[8,16,16]{2,1,0:T(8,128)S(1)}, f32[8,16,16]{2,1,0:T(8,128)}, u32[]{:S(2)}) copy-start(f32[8,16,16]{2,1,0:T(8,128)} %param.11) | copy-start | bytes 24580
  0.6 1.2 copy-start.1
  1.9 35.2 %copy-start.9 = (f32[1,128,128]{2,1,0:T(8,128)S(1)}, f32[1,128,128]{2,1,0:T(8,128)}, u32[]{:S(2)}) copy-start(f32[1,128,128]{2,1,0:T(8,128)} %param.10) | copy-start | bytes 196612
  37.0 0.7 copy-start.10
  39.4 3.7 %copy-start.2 = (f32[128,1024]{1,0:T(8,128)S(1)}, f32[128,1024]{1,0:T(8,128)}, u32[]{:S(2)}) copy-start(f32[128,1024]{1,0:T(8,128)} %param.8) | copy-start | bytes 1572868
  39.4 3.7 %copy-start.8 = (f32[8,16,16]{2,1,0:T(8,128)S(1)}, f32[8,16,16]{2,1,0:T(8,128)}, u32[]{:S(2)}) copy-start(f32[8,16,16]{2,1,0:T(8,128)} %param.13) | copy-start | bytes 24580
  39.4 17.9 %all-to-all-start = ((f32[1,128,1024]{2,0,1:T(1,128)}), f32[1,128,1024]{2,0,1:T(1,128)S(1)}, u32[]{:S(2)}, u32[]{:S(2)}) async-start(f32[1,128,1024]{2,0,1:T(1,128)} %copy.50), calls=%async_computation | async-start | bytes 1048576 | tf_op jit(solution)/shard_map/all_to_all | solution.py:29
  57.3 18.4 %all-to-all-start.2 = ((f32[16,8,1024]{2,1,0:T(8,128)}), f32[16,8,1024]{2,1,0:T(8,128)S(1)}, u32[]{:S(2)}, u32[]{:S(2)}) async-start(f32[16,8,1024]{2,1,0:T(8,128)} %copy.56), calls=%async_computation.2 | async-start | bytes 1048576 | tf_op jit(solution)/shard_map/all_to_all | solution.py:37
  61.5 1.8 %copy-start.3 = (f32[1,128,1024]{2,1,0:T(8,128)}, f32[1,128,1024]{2,1,0:T(8,128)S(1)}, u32[]{:S(2)}) copy-start(f32[1,128,1024]{2,1,0:T(8,128)S(1)} %copy.79) | copy-start | bytes 1572868
  61.5 1.8 %copy-start.7 = (f32[1,128,128]{2,1,0:T(8,128)S(1)}, f32[1,128,128]{2,1,0:T(8,128)}, u32[]{:S(2)}) copy-start(f32[1,128,128]{2,1,0:T(8,128)} %param.12) | copy-start | bytes 196612
  75.7 18.5 %all-to-all-start.1 = ((f32[1,128,1024]{2,0,1:T(1,128)}), f32[1,128,1024]{2,0,1:T(1,128)}, u32[]{:S(2)}, u32[]{:S(2)}) async-start(f32[1,128,1024]{2,0,1:T(1,128)} %copy.53), calls=%async_computation.1 | async-start | bytes 1048576 | tf_op jit(solution)/shard_map/all_to_all | solution.py:29
  80.1 1.0 copy-start.5
  80.8 1.3 copy-start.6
  84.4 14.0 %copy-start.4 = (f32[1,128,1024]{2,1,0:T(8,128)S(1)}, f32[1,128,1024]{2,1,0:T(8,128)}, u32[]{:S(2)}) copy-start(f32[1,128,1024]{2,1,0:T(8,128)} %copy-done.3) | copy-start | bytes 1572868
  94.2 18.4 %all-to-all-start.3 = ((f32[16,8,1024]{2,1,0:T(8,128)}), f32[16,8,1024]{2,1,0:T(8,128)S(1)}, u32[]{:S(2)}, u32[]{:S(2)}) async-start(f32[16,8,1024]{2,1,0:T(8,128)} %copy.57), calls=%async_computation.3 | async-start | bytes 1048576 | tf_op jit(solution)/shard_map/all_to_all | solution.py:37
